TPU v7x, 32 devices: a whole 2x2x4 slice. The times are simulated.
32 devices in a mesh: tensor: 4 (over z), frames: 2 (over core), batch: 4 (over y, x).
Axes of the slice: x: 2, y: 2, z: 4, core: 2. Of those that a mesh axis runs over, the one named last changes fastest.
Arguments:
- tokens: bfloat16 [4, 2, 1024, 1024], P('batch', 'frames', 'tensor'), may hold values from -6 to 6
- cotangent: bfloat16 [4, 2, 1024, 1024], P('batch', 'frames', 'tensor'), may hold values from -6 to 6
- bucket: int32 [4], P('batch'), may hold values from 0 to 1, as said below
- clip_of_frame: int32 [4, 8], P('batch'), may hold values from 0 to 6, as said below
- noise_index: int32 [4, 8], P('batch'), may hold values from 0 to 999
- noise_table: float32 [1000, 1024], replicated, may hold values from -6 to 6
- w_mod: bfloat16 [1024, 6144], P(None, 'tensor'), may hold values from -0.1875 to 0.1875
- b_mod: bfloat16 [6144], P('tensor'), may hold values from -1.796875 to 1.796875
- w_qkv: bfloat16 [1024, 3, 1024], P(None, None, 'tensor'), may hold values from -0.1875 to 0.1875
- w_out: bfloat16 [1024, 1024], P('tensor'), may hold values from -1 to 1
- w_up: bfloat16 [1024, 4096], P(None, 'tensor'), may hold values from -0.1875 to 0.1875
- w_down: bfloat16 [4096, 1024], P('tensor'), may hold values from -0.09375 to 0.09375
Outputs:
- out: bfloat16 [4, 2, 1024, 1024], P('batch', 'frames', 'tensor')
- d_tokens: bfloat16 [4, 2, 1024, 1024], P('batch', 'frames', 'tensor')
- d_w_mod: float32 [1024, 6144], P(None, 'tensor')
- d_b_mod: float32 [6144], P('tensor')
- d_w_qkv: float32 [1024, 3, 1024], P(None, None, 'tensor')
- d_w_out: float32 [1024, 1024], P('tensor')
- d_w_up: float32 [1024, 4096], P(None, 'tensor')
- d_w_down: float32 [4096, 1024], P('tensor')
Inputs may be any that keep to these rules, and one draw needn't show every extreme that they name: `bucket`: both values occur in every draw. `clip_of_frame`: A row starts at 0 and never falls; with F the row's frame count (2048 divided by its frame size), frames F // 2 - 1 and F // 2 share a clip; entries from frame F on repeat the clip of frame F - 1. In some pack of 16 by 16 patches every other frame starts a clip of its own. `noise_index`: only a row's first 2048 / (frame size) entries are read.
All inputs are finite; a program needn't handle non-finite values.
Results may differ from a plain program's by a relative error of at most 0.017.
The roundings to bfloat16 on the way count: a program that leaves them out, or rounds other values in their place, can miss the bound.
Values may be sent and summed in bfloat16 or wider, within the bound.
No kernel may reach another device: no remote copies, remote signals or barrier semaphores. Data moves between devices by JAX's collectives and lax.ppermute only.
A program may use at most 192 MiB of HBM per device.

v0:
```python
import jax
import jax.numpy as jnp
from jax import lax
from jax.sharding import PartitionSpec as P

HEAD_DIM = 64
FRAME_SMALL = 256
FRAME_LARGE = 1024
eps = 1e-06
highest = lax.Precision.HIGHEST


def from_behind(value, axis, steps):
    count = lax.axis_size(axis)
    initial, last = (max(0, -steps), min(count, count - steps))
    return lax.ppermute(value, axis, [(source, source + steps) for source in range(initial, last)])


def normalize(values):
    centre = values - jnp.mean(values, axis=-1, keepdims=True)
    spread = jnp.mean(centre * centre, axis=-1, keepdims=True)
    inverse = lax.rsqrt(spread + eps)
    return (centre * inverse, inverse)


def norm_back(grad, normed, inverse):
    mean_grad = jnp.mean(grad, axis=-1, keepdims=True)
    mean_mix = jnp.mean(grad * normed, axis=-1, keepdims=True)
    return inverse * (grad - mean_grad - normed * mean_mix)


def rotary(positions):
    half_dim = HEAD_DIM // 2
    frequency = 10000.0 ** (-(jnp.arange(half_dim, dtype=jnp.float32) * 2.0 / HEAD_DIM))
    angles = positions.astype(jnp.float32)[:, None] * frequency[None, :]
    cosine = jnp.concatenate([jnp.cos(angles), jnp.cos(angles)], axis=-1)[:, None, :]
    sine_table = jnp.concatenate([jnp.sin(angles), jnp.sin(angles)], axis=-1)[:, None, :]
    return (cosine, sine_table)


def rotate(values, cosine, sine_table):
    half_dim = values.shape[-1] // 2
    turned = jnp.concatenate([-values[..., half_dim:], values[..., :half_dim]], axis=-1)
    return values * cosine + turned * sine_table


def gelu_back(pre, grad_hidden):
    return jax.vjp(lambda inner: jax.nn.gelu(inner, approximate=True), pre)[1](grad_hidden)[0]


def spread_rows(rows):
    return lax.all_gather(rows, "tensor", axis=0, tiled=True)


def collect_rows(left_rows, right_matrix, contract):
    return lax.psum_scatter(
        lax.dot_general(
            left_rows,
            right_matrix,
            (((1,), (contract,)), ((), ())),
            preferred_element_type=jnp.float32,
        ),
        "tensor",
        scatter_dimension=0,
        tiled=True,
    )


def masked_scores(query_block, frame_query, clip_query, all_keys, key_frame, key_clip, score_scale):
    allowed = (clip_query[:, None] == key_clip[None, :]) & (
        key_frame[None, :] <= frame_query[:, None]
    )
    scores = (
        jnp.einsum("qhd,khd->hqk", query_block, all_keys, preferred_element_type=jnp.float32)
        * score_scale
    )
    return jnp.where(allowed[None], scores, -1e30)


def attend(
    query_block, frame_query, clip_query, all_keys, all_values, key_frame, key_clip, score_scale
):
    scores = masked_scores(
        query_block, frame_query, clip_query, all_keys, key_frame, key_clip, score_scale
    )
    row_max = jnp.max(scores, axis=-1, keepdims=True)
    weights_exp = jnp.exp(scores - row_max)
    row_total = jnp.sum(weights_exp, axis=-1, keepdims=True)
    probabilities = (weights_exp / row_total).astype(jnp.bfloat16)
    mixed = jnp.einsum(
        "hqk,khd->qhd", probabilities, all_values, preferred_element_type=jnp.float32
    )
    return (mixed, (row_max + jnp.log(row_total))[..., 0])


def attend_back(
    query_block,
    frame_query,
    clip_query,
    grad_mixed,
    log_total,
    all_keys,
    all_values,
    key_frame,
    key_clip,
    score_scale,
):
    scores = masked_scores(
        query_block, frame_query, clip_query, all_keys, key_frame, key_clip, score_scale
    )
    probabilities = jnp.exp(scores - log_total[..., None])
    grad_probs = jnp.einsum(
        "qhd,khd->hqk", grad_mixed, all_values, preferred_element_type=jnp.float32
    )
    centre = jnp.sum(probabilities * grad_probs, axis=-1, keepdims=True)
    grad_scores = (probabilities * (grad_probs - centre)).astype(jnp.bfloat16)
    grad_query = (
        jnp.einsum("hqk,khd->qhd", grad_scores, all_keys, preferred_element_type=jnp.float32)
        * score_scale
    )
    grad_keys = (
        jnp.einsum("hqk,qhd->khd", grad_scores, query_block, preferred_element_type=jnp.float32)
        * score_scale
    )
    grad_values = jnp.einsum(
        "hqk,qhd->khd",
        probabilities.astype(jnp.bfloat16),
        grad_mixed,
        preferred_element_type=jnp.float32,
    )
    return (grad_query, grad_keys, grad_values)


def local(
    tokens,
    cotangent,
    bucket,
    clip_of_frame,
    noise_index,
    noise_table,
    w_mod,
    b_mod,
    w_qkv,
    w_out,
    w_up,
    w_down,
):
    tensor_size = lax.axis_size("tensor")
    tensor_rank = lax.axis_index("tensor")
    frame_rank = lax.axis_index("frames")
    local_rows = tokens.shape[2]
    model_width = tokens.shape[3]
    shard_rows = local_rows * tensor_size
    width_local = w_qkv.shape[2]
    heads_local = width_local // HEAD_DIM
    frame_slots = clip_of_frame.shape[1]
    clip_row = clip_of_frame[0]
    level_row = noise_index[0]
    frame_size = jnp.where(bucket[0] == 0, FRAME_SMALL, FRAME_LARGE).astype(jnp.int32)
    shard_start = frame_rank * shard_rows
    shard_pos = shard_start + jnp.arange(shard_rows, dtype=jnp.int32)
    local_pos = shard_start + tensor_rank * local_rows + jnp.arange(local_rows, dtype=jnp.int32)
    local_frame = local_pos // frame_size
    shard_frame = shard_pos // frame_size
    shard_clip = jnp.take(clip_row, shard_frame)
    past_pos = shard_pos - shard_rows
    past_frame = jnp.maximum(past_pos, 0) // frame_size
    past_clip = jnp.where(past_pos >= 0, jnp.take(clip_row, past_frame), -1)
    key_frame = jnp.concatenate([past_frame, shard_frame])
    key_clip = jnp.concatenate([past_clip, shard_clip])
    cond = jax.nn.silu(jnp.take(noise_table, level_row, axis=0)).astype(jnp.bfloat16)
    mod_part = (
        jnp.dot(cond, w_mod, preferred_element_type=jnp.float32)
        + b_mod.astype(jnp.float32)[None, :]
    )
    mod_whole = lax.all_gather(mod_part, "tensor", axis=1, tiled=True)
    selector = (local_frame[:, None] == jnp.arange(frame_slots, dtype=jnp.int32)[None, :]).astype(
        jnp.float32
    )
    per_token = jnp.dot(selector, mod_whole, precision=highest)
    shift_one = per_token[:, 0:model_width]
    scale_one = per_token[:, model_width : 2 * model_width]
    gate_one = per_token[:, 2 * model_width : 3 * model_width]
    shift_two = per_token[:, 3 * model_width : 4 * model_width]
    scale_two = per_token[:, 4 * model_width : 5 * model_width]
    gate_two = per_token[:, 5 * model_width : 6 * model_width]
    residual = tokens[0, 0].astype(jnp.float32)
    normed_one, inverse_one = normalize(residual)
    attn_in = (normed_one * (1.0 + scale_one) + shift_one).astype(jnp.bfloat16)
    attn_whole = spread_rows(attn_in)
    projected = jnp.einsum("sd,dcf->scf", attn_whole, w_qkv, preferred_element_type=jnp.float32)
    cosine, sine_table = rotary(shard_pos)
    q_raw = projected[:, 0].reshape(shard_rows, heads_local, HEAD_DIM)
    k_raw = projected[:, 1].reshape(shard_rows, heads_local, HEAD_DIM)
    queries = rotate(q_raw, cosine, sine_table).astype(jnp.bfloat16)
    own_keys = rotate(k_raw, cosine, sine_table).astype(jnp.bfloat16)
    own_values = projected[:, 2].reshape(shard_rows, heads_local, HEAD_DIM).astype(jnp.bfloat16)
    past_keys, past_values = from_behind((own_keys, own_values), "frames", 1)
    all_keys = jnp.concatenate([past_keys, own_keys], axis=0)
    all_values = jnp.concatenate([past_values, own_values], axis=0)
    score_scale = HEAD_DIM ** (-0.5)
    block_rows = min(512, shard_rows)
    block_count = shard_rows // block_rows
    query_blocks = queries.reshape(block_count, block_rows, heads_local, HEAD_DIM)
    frame_blocks = shard_frame.reshape(block_count, block_rows)
    clip_blocks = shard_clip.reshape(block_count, block_rows)

    def forward_block(block_items):
        return attend(
            block_items[0],
            block_items[1],
            block_items[2],
            all_keys,
            all_values,
            key_frame,
            key_clip,
            score_scale,
        )

    attn_blocks, total_blocks = lax.map(forward_block, (query_blocks, frame_blocks, clip_blocks))
    attn_rows = attn_blocks.reshape(shard_rows, width_local).astype(jnp.bfloat16)
    branch_one = collect_rows(attn_rows, w_out, 0)
    mixed_one = residual + gate_one * branch_one
    normed_two, inverse_two = normalize(mixed_one)
    mlp_in = (normed_two * (1.0 + scale_two) + shift_two).astype(jnp.bfloat16)
    mlp_whole = spread_rows(mlp_in)
    pre = jnp.dot(mlp_whole, w_up, preferred_element_type=jnp.float32)
    hidden = jax.nn.gelu(pre, approximate=True).astype(jnp.bfloat16)
    branch_two = collect_rows(hidden, w_down, 0)
    result = (mixed_one + gate_two * branch_two).astype(jnp.bfloat16)
    grad_out = cotangent[0, 0].astype(jnp.float32)
    grad_branch_two = (gate_two * grad_out).astype(jnp.bfloat16)
    grad_gate_two = grad_out * branch_two
    grad_two_whole = spread_rows(grad_branch_two)
    mlp_source, _ = lax.optimization_barrier((mlp_in, grad_branch_two))
    mlp_again = spread_rows(mlp_source)
    grad_hidden = lax.dot_general(
        grad_two_whole, w_down, (((1,), (1,)), ((), ())), preferred_element_type=jnp.float32
    )
    grad_pre = gelu_back(pre, grad_hidden).astype(jnp.bfloat16)
    grad_w_down = lax.dot_general(
        hidden, grad_two_whole, (((0,), (0,)), ((), ())), preferred_element_type=jnp.float32
    )
    grad_w_up = lax.dot_general(
        mlp_again, grad_pre, (((0,), (0,)), ((), ())), preferred_element_type=jnp.float32
    )
    grad_mlp_in = collect_rows(grad_pre, w_up, 1)
    grad_scale_two = grad_mlp_in * normed_two
    grad_mixed_one = grad_out + norm_back(grad_mlp_in * (1.0 + scale_two), normed_two, inverse_two)
    grad_branch_one = (gate_one * grad_mixed_one).astype(jnp.bfloat16)
    grad_gate_one = grad_mixed_one * branch_one
    grad_one_whole = spread_rows(grad_branch_one)
    grad_attn = lax.dot_general(
        grad_one_whole, w_out, (((1,), (1,)), ((), ())), preferred_element_type=jnp.float32
    ).astype(jnp.bfloat16)
    grad_w_out = lax.dot_general(
        attn_rows, grad_one_whole, (((0,), (0,)), ((), ())), preferred_element_type=jnp.float32
    )
    grad_attn_blocks = grad_attn.reshape(block_count, block_rows, heads_local, HEAD_DIM)

    def backward_block(carry, block_items):
        query_block, frame_query, clip_query, grad_mixed, log_total = block_items
        grad_query, grad_keys, grad_values = attend_back(
            query_block,
            frame_query,
            clip_query,
            grad_mixed,
            log_total,
            all_keys,
            all_values,
            key_frame,
            key_clip,
            score_scale,
        )
        return ((carry[0] + grad_keys, carry[1] + grad_values), grad_query)

    zero_keys = jnp.zeros((2 * shard_rows, heads_local, HEAD_DIM), jnp.float32)
    key_sums, query_grads = lax.scan(
        backward_block,
        (zero_keys, zero_keys),
        (query_blocks, frame_blocks, clip_blocks, grad_attn_blocks, total_blocks),
    )
    back_keys, back_values = (
        from_behind(key_sums[0][:shard_rows].astype(jnp.bfloat16), "frames", -1).astype(
            jnp.float32
        ),
        from_behind(key_sums[1][:shard_rows].astype(jnp.bfloat16), "frames", -1).astype(
            jnp.float32
        ),
    )
    own_key_grads = key_sums[0][shard_rows:] + back_keys
    own_value_grads = key_sums[1][shard_rows:] + back_values
    grad_q_raw = rotate(query_grads.reshape(shard_rows, heads_local, HEAD_DIM), cosine, -sine_table)
    grad_k_raw = rotate(own_key_grads, cosine, -sine_table)
    grad_qkv = jnp.stack(
        [
            grad_q_raw.reshape(shard_rows, width_local),
            grad_k_raw.reshape(shard_rows, width_local),
            own_value_grads.reshape(shard_rows, width_local),
        ],
        axis=1,
    ).astype(jnp.bfloat16)
    attn_source, _ = lax.optimization_barrier((attn_in, grad_attn))
    attn_again = spread_rows(attn_source)
    grad_w_qkv = jnp.einsum("sd,scf->dcf", attn_again, grad_qkv, preferred_element_type=jnp.float32)
    grad_attn_in = collect_rows(
        grad_qkv.reshape(shard_rows, 3 * width_local),
        w_qkv.reshape(model_width, 3 * width_local),
        1,
    )
    grad_scale_one = grad_attn_in * normed_one
    grad_tokens = grad_mixed_one + norm_back(
        grad_attn_in * (1.0 + scale_one), normed_one, inverse_one
    )
    grad_token_mod = jnp.concatenate(
        [grad_attn_in, grad_scale_one, grad_gate_one, grad_mlp_in, grad_scale_two, grad_gate_two],
        axis=1,
    )
    grad_frame_mod = lax.dot_general(
        selector, grad_token_mod, (((0,), (0,)), ((), ())), precision=highest
    )
    mod_share = lax.psum_scatter(
        grad_frame_mod.astype(jnp.bfloat16), "tensor", scatter_dimension=1, tiled=True
    ).astype(jnp.float32)
    grad_w_mod = lax.dot_general(
        cond.astype(jnp.float32), mod_share, (((0,), (0,)), ((), ())), precision=highest
    )
    grad_b_mod = jnp.sum(mod_share, axis=0)
    summed = (
        lax.psum(grad_w_mod.astype(jnp.bfloat16), ("frames", "batch")).astype(jnp.float32),
        lax.psum(grad_b_mod.astype(jnp.bfloat16), ("frames", "batch")).astype(jnp.float32),
        lax.psum(grad_w_qkv.astype(jnp.bfloat16), ("frames", "batch")).astype(jnp.float32),
        lax.psum(grad_w_out.astype(jnp.bfloat16), ("frames", "batch")).astype(jnp.float32),
        lax.psum(grad_w_up.astype(jnp.bfloat16), ("frames", "batch")).astype(jnp.float32),
        lax.psum(grad_w_down.astype(jnp.bfloat16), ("frames", "batch")).astype(jnp.float32),
    )
    return (
        result.reshape(1, 1, local_rows, model_width),
        grad_tokens.astype(jnp.bfloat16).reshape(1, 1, local_rows, model_width),
        summed[0],
        summed[1],
        summed[2],
        summed[3],
        summed[4],
        summed[5],
    )


def solution(mesh):
    placed = (
        P("batch", "frames", "tensor", None),
        P("batch", "frames", "tensor", None),
        P("batch"),
        P("batch", None),
        P("batch", None),
        P(),
        P(None, "tensor"),
        P("tensor"),
        P(None, None, "tensor"),
        P("tensor", None),
        P(None, "tensor"),
        P("tensor", None),
    )
    return jax.shard_map(
        local,
        mesh=mesh,
        in_specs=placed,
        out_specs=(
            P("batch", "frames", "tensor", None),
            P("batch", "frames", "tensor", None),
            P(None, "tensor"),
            P("tensor"),
            P(None, None, "tensor"),
            P("tensor", None),
            P(None, "tensor"),
            P("tensor", None),
        ),
        check_vma=False,
    )
```

profile of v0, /device:TPU:0, one launch (start us, length us, event | category | flops | bytes accessed | tf_op | source)
XLA Modules:
  0.0 981.8 jit_solution(5190104987393337398)
XLA Ops:
  16.0 15.6 %all_gather.21 = f32[8,6144]{1,0:T(8,128)S(1)} all-gather(f32[8,1536]{1,0:T(8,128)S(1)} %convolution_add_fusion), channel_id=1, replica_groups=mesh['tensor'=4,'frames'=2,'batch'=4] {'tensor'}, dimensions={1}, use_global_device_ids=true | all-gather | bytes 245760 | tf_op jit(solution)/shard_map/all_gather | solution.py:176
  51.4 34.1 %all-gather.7.cloned.1.call-done = bf16[1024,1024]{1,0:T(8,128)(2,1)} async-done(((bf16[256,1024]{1,0:T(8,128)(2,1)}), bf16[1024,1024]{1,0:T(8,128)(2,1)}) %all-gather.7.cloned.1.call-update) | async-done | bytes 2097168 | tf_op jit(solution)/shard_map/all_gather | solution.py:52
  104.5 29.2 %while.29 = (s32[]{:T(128)}, bf16[2,512,4,64]{1,3,2,0:T(8,128)(2,1)S(1)}, f32[2,4,512]{2,1,0:T(4,128)}, s32[2,512]{1,0:T(2,128)S(1)}, s32[2048]{0:T(1024)S(1)}, ...) while((s32[]{:T(128)}, ...), condition=%wide.region_5.7_spmd.clone, body=%wide.region_2.6_spmd.sunk.clone | while | flops 1127217152 | bytes 57503868 | solution.py:220
  139.0 75.9 %reduce-scatter.6.cloned.1.call-done = f32[256,1024]{1,0:T(8,128)} async-done(((f32[1024,1024]{1,0:T(8,128)}), f32[256,1024]{1,0:T(8,128)}) %reduce-scatter.6.cloned.1.call-update) | async-done | bytes 1048592 | tf_op jit(solution)/shard_map/reduce_scatter | solution.py:56
  221.9 45.3 %all-gather.11.cloned.1.call-done = bf16[1024,1024]{1,0:T(8,128)(2,1)} async-done(((bf16[256,1024]{1,0:T(8,128)(2,1)}), bf16[1024,1024]{1,0:T(8,128)(2,1)}) %all-gather.11.cloned.1.call-update) | async-done | bytes 2097168 | tf_op jit(solution)/shard_map/all_gather | solution.py:52
  273.8 39.3 %all-gather.9.cloned.1.call-done = bf16[1024,1024]{1,0:T(8,128)(2,1)} async-done(((bf16[256,1024]{1,0:T(8,128)(2,1)}), bf16[1024,1024]{1,0:T(8,128)(2,1)}) %all-gather.9.cloned.1.call-update) | async-done | bytes 2097168 | tf_op jit(solution)/shard_map/all_gather | solution.py:52
  313.1 10.0 %fusion.47 = (bf16[1024,1024]{1,0:T(8,128)(2,1)S(1)}, f32[1024,1024]{1,0:T(8,128)}) fusion(f32[1024,1024]{1,0:T(8,128)} %fusion.107, bf16[1024,1024]{1,0:T(8,128)(2,1)} %all-gather.9.cloned.1.call-done, bf16[1024,1024]{1,0:T(8,128)(2,1)} %param.28), kind=kOutput, calls=%fused_computation.62 | convolution fusion | flops 2168455168 | bytes 14680064 | tf_op jit(solution)/shard_map/dot_general | solution.py:227
  328.9 7.5 fusion.101
  336.5 68.1 %reduce-scatter.10.cloned.1.call-done = f32[256,1024]{1,0:T(8,128)} async-done(((f32[1024,1024]{1,0:T(8,128)}), f32[256,1024]{1,0:T(8,128)}) %reduce-scatter.10.cloned.1.call-update) | async-done | bytes 1048592 | tf_op jit(solution)/shard_map/reduce_scatter | solution.py:56
  406.8 77.3 %reduce-scatter.8.cloned.1.call-done = f32[256,1024]{1,0:T(8,128)} async-done(((f32[1024,1024]{1,0:T(8,128)}), f32[256,1024]{1,0:T(8,128)}) %reduce-scatter.8.cloned.1.call-update) | async-done | bytes 1048592 | tf_op jit(solution)/shard_map/reduce_scatter | solution.py:56
  489.6 45.5 %all-gather.13.cloned.1.call-done = bf16[1024,1024]{1,0:T(8,128)(2,1)} async-done(((bf16[256,1024]{1,0:T(8,128)(2,1)}), bf16[1024,1024]{1,0:T(8,128)(2,1)}) %all-gather.13.cloned.1.call-update) | async-done | bytes 2097168 | tf_op jit(solution)/shard_map/all_gather | solution.py:52
  541.2 94.7 %while.30 = (s32[]{:T(128)}, f32[2048,4,64]{0,2,1:T(8,128)}, f32[2048,4,64]{0,2,1:T(8,128)}, f32[2,512,4,64]{1,3,2,0:T(8,128)}, bf16[2,512,4,64]{1,3,2,0:T(8,128...) while((s32[]{:T(128)}, f32[2048,4,64]{0,2,1:T(8,128)}, ...), condition=%wide.region_15.17_spmd.clone.clone, body=%wide.region_13.16_spmd.clone.sunk.clone | while | flops 2753165312 | bytes 195776976 | solution.py:278
  554.4 11.6 %multiply_reduce_fusion.5 = (f32[4,512]{1,0:T(4,128)}, f32[4,512,2048]{2,1,0:T(8,128)}) fusion(f32[4,512,2048]{2,1,0:T(8,128)S(1)} %fusion.188, f32[4,512]{1,0:T(4,128)S(1)} %dynamic-slice_bitcast_fusion.3, pred[512,2048]{1,0:T(8,128)(4,1)} %copy-done.3, bf16[2048,4,64]{0,2,1:T(8,128)(2,1)} %copy-done.8, ...), kind=kOutput, calls=%fused_computation.20.clone.1.clone | convolution fusion | flops 557840384 | bytes 35930116 | tf_op jit(solution)/shard_map/while/body/eval_jaxpr/qhd,khd->hqk/dot_general | solution.py:112
  566.0 11.0 %multiply_convert_fusion.10 = bf16[4,512,2048]{2,1,0:T(8,128)(2,1)} fusion(f32[4,512,2048]{2,1,0:T(8,128)} %get-tuple-element.524, f32[4,512,2048]{2,1,0:T(8,128)S(1)} %fusion.188, f32[4,512]{1,0:T(4,128)} %get-tuple-element.525, f32[4,512]{1,0:T(4,128)S(1)} %dynamic-slice_bitcast_fusion.3, pred[512,2048]{1,0:T(8,128)(4,1)} %copy-done.3), kind=kLoop, calls=%fused_computation.19.clone.1.clone | loop fusion | flops 25165824 | bytes 43008000 | tf_op jit(solution)/shard_map/while/body/eval_jaxpr/convert_element_type | solution.py:116
  577.1 7.1 fusion.191
  593.9 7.5 fusion.190
  601.4 11.6 %multiply_reduce_fusion.5 = (f32[4,512]{1,0:T(4,128)}, f32[4,512,2048]{2,1,0:T(8,128)}) fusion(f32[4,512,2048]{2,1,0:T(8,128)S(1)} %fusion.188, f32[4,512]{1,0:T(4,128)S(1)} %dynamic-slice_bitcast_fusion.3, pred[512,2048]{1,0:T(8,128)(4,1)} %copy-done.3, bf16[2048,4,64]{0,2,1:T(8,128)(2,1)} %copy-done.8, ...), kind=kOutput, calls=%fused_computation.20.clone.1.clone | convolution fusion | flops 557840384 | bytes 35930116 | tf_op jit(solution)/shard_map/while/body/eval_jaxpr/qhd,khd->hqk/dot_general | solution.py:112
  613.0 11.0 %multiply_convert_fusion.10 = bf16[4,512,2048]{2,1,0:T(8,128)(2,1)} fusion(f32[4,512,2048]{2,1,0:T(8,128)} %get-tuple-element.524, f32[4,512,2048]{2,1,0:T(8,128)S(1)} %fusion.188, f32[4,512]{1,0:T(4,128)} %get-tuple-element.525, f32[4,512]{1,0:T(4,128)S(1)} %dynamic-slice_bitcast_fusion.3, pred[512,2048]{1,0:T(8,128)(4,1)} %copy-done.3), kind=kLoop, calls=%fused_computation.19.clone.1.clone | loop fusion | flops 25165824 | bytes 43008000 | tf_op jit(solution)/shard_map/while/body/eval_jaxpr/convert_element_type | solution.py:116
  624.0 7.0 fusion.191
  688.8 60.6 %reduce-scatter.12.cloned.1.call-done = f32[256,1024]{1,0:T(8,128)} async-done(((f32[1024,1024]{1,0:T(8,128)}), f32[256,1024]{1,0:T(8,128)}) %reduce-scatter.12.cloned.1.call-update) | async-done | bytes 1048592 | tf_op jit(solution)/shard_map/reduce_scatter | solution.py:56
  758.7 38.2 %all-gather.15.cloned.1.call-done = bf16[1024,1024]{1,0:T(8,128)(2,1)} async-done(((bf16[256,1024]{1,0:T(8,128)(2,1)}), bf16[1024,1024]{1,0:T(8,128)(2,1)}) %all-gather.15.cloned.1.call-update) | async-done | bytes 2097168 | tf_op jit(solution)/shard_map/all_gather | solution.py:52
  801.6 16.4 %reduce-scatter.14.cloned.1.call-done = bf16[8,1536]{1,0:T(8,128)(2,1)} async-done(((bf16[8,6144]{1,0:T(8,128)(2,1)}), bf16[8,1536]{1,0:T(8,128)(2,1)}) %reduce-scatter.14.cloned.1.call-update) | async-done | bytes 24592 | tf_op jit(solution)/shard_map/reduce_scatter | solution.py:322
  822.3 15.2 %psum.43 = bf16[1536]{0:T(1024)(128)(2,1)S(1)} all-reduce(bf16[1536]{0:T(1024)(128)(2,1)S(1)} %reduce_sum.110), channel_id=1, replica_groups=mesh['tensor'=4,'frames'=2,'batch'=4] {'frames','batch'}, use_global_device_ids=true, to_apply=%region_22.24 | all-reduce | flops 1536 | bytes 6144 | tf_op jit(solution)/shard_map/psum | solution.py:331
  838.1 121.2 %all-reduce.3.cloned.1.call-done = (bf16[1024,1536]{1,0:T(8,128)(2,1)}, bf16[1024,3,256]{2,0,1:T(8,128)(2,1)}, bf16[256,1024]{1,0:T(8,128)(2,1)}, bf16[1024,1024]{1,0:T(8,128)(2,1)}, bf16[1024,1024]{1,0:T(8,128)(2,1)}) async-done(((bf16[1024,1536]{1,0:T(8,128)(2,1)}, bf16[1024,3,256]{2,0,1:T(8,128)(2,1)}, bf16[256,1024]{1,0:T(8,128)(2,1)}, bf16[1024,1024]{1,0:T(8,128)(2,1)}, bf16[1024,1024]{1,0:T(8,128)(2,1)}), ...) | async-done | bytes 9437200 | tf_op jit(solution)/shard_map/psum | solution.py:330
  (314 shorter events, 227.9 us)
Async XLA Ops:
  7.2 78.3 %all-gather.7.cloned.1.call-start = ((), (), s32[]{:S(2)}) async-start(), calls=%async_computation.5 | async-start | bytes 2621440 | tf_op jit(solution)/shard_map/all_gather | solution.py:52
  38.4 176.6 %reduce-scatter.6.cloned.1.call-start = ((), (), s32[]{:S(2)}) async-start(), calls=%async_computation.6 | async-start | bytes 5242880 | tf_op jit(solution)/shard_map/reduce_scatter | solution.py:56
  90.1 13.0 %collective-permute-start.1 = (bf16[1024,4,64]{0,2,1:T(8,128)(2,1)}, bf16[1024,4,64]{0,2,1:T(8,128)(2,1)}, u32[]{:S(2)}, u32[]{:S(2)}) collective-permute-start(bf16[1024,4,64]{0,2,1:T(8,128)(2,1)} %bitcast.31), channel_id=1, source_target_pairs={{0,4},{1,5},{2,6},{3,7},{8,12},{9,13},{10,14},{11,15},{16,20},{17,... | collective-permute-start | bytes 1572872 | tf_op jit(solution)/shard_map/ppermute | solution.py:16
  99.5 4.8 collective-permute-start
  138.9 76.0 %copy-start.13 = (bf16[1,1,256,1024]{3,2,1,0:T(8,128)(2,1)S(1)}, bf16[1,1,256,1024]{3,2,1,0:T(8,128)(2,1)}, u32[]{:S(2)}) copy-start(bf16[1,1,256,1024]{3,2,1,0:T(8,128)(2,1)} %param.18) | copy-start | bytes 1572868
  138.9 128.2 %all-gather.11.cloned.1.call-start = ((), (), s32[]{:S(2)}) async-start(), calls=%async_computation.9 | async-start | bytes 2621440 | tf_op jit(solution)/shard_map/all_gather | solution.py:52
  216.7 267.3 %copy-start.51 = (f32[256]{0:T(256)}, f32[256]{0:T(256)S(1)}, u32[]{:S(2)}) copy-start(f32[256]{0:T(256)S(1)} %broadcast_multiply_fusion.4) | copy-start | bytes 3076
  217.7 266.4 %copy-start.56 = (f32[256]{0:T(256)}, f32[256]{0:T(256)S(1)}, u32[]{:S(2)}) copy-start(f32[256]{0:T(256)S(1)} %add_rsqrt_fusion) | copy-start | bytes 3076
  220.8 92.2 %all-gather.9.cloned.1.call-start = ((), (), s32[]{:S(2)}) async-start(), calls=%async_computation.7 | async-start | bytes 2621440 | tf_op jit(solution)/shard_map/all_gather | solution.py:52
  221.4 183.2 %reduce-scatter.10.cloned.1.call-start = ((), (), s32[]{:S(2)}) async-start(), calls=%async_computation.10 | async-start | bytes 5242880 | tf_op jit(solution)/shard_map/reduce_scatter | solution.py:56
  328.8 155.2 %reduce-scatter.8.cloned.1.call-start = ((), (), s32[]{:S(2)}) async-start(), calls=%async_computation.8 | async-start | bytes 5242880 | tf_op jit(solution)/shard_map/reduce_scatter | solution.py:56
  336.4 147.7 %copy-start.19 = (bf16[1,1,256,1024]{3,2,1,0:T(8,128)(2,1)S(1)}, bf16[1,1,256,1024]{3,2,1,0:T(8,128)(2,1)}, u32[]{:S(2)}) copy-start(bf16[1,1,256,1024]{3,2,1,0:T(8,128)(2,1)} %param.19) | copy-start | bytes 1572868
  336.4 198.7 %all-gather.13.cloned.1.call-start = ((), (), s32[]{:S(2)}) async-start(), calls=%async_computation.11 | async-start | bytes 2621440 | tf_op jit(solution)/shard_map/all_gather | solution.py:52
  488.8 190.8 %all-gather.17.cloned.1.call-start = ((), (), s32[]{:S(2)}) async-start(), calls=%async_computation.15 | async-start | bytes 2621440 | tf_op jit(solution)/shard_map/all_gather | solution.py:52
  489.6 259.8 %reduce-scatter.12.cloned.1.call-start = ((), (), s32[]{:S(2)}) async-start(), calls=%async_computation.12 | async-start | bytes 5242880 | tf_op jit(solution)/shard_map/reduce_scatter | solution.py:56
  638.2 15.6 %collective-permute-start.3 = (bf16[1024,4,64]{0,2,1:T(8,128)(2,1)}, bf16[1024,4,64]{0,2,1:T(8,128)(2,1)}, u32[]{:S(2)}, u32[]{:S(2)}) collective-permute-start(bf16[1024,4,64]{0,2,1:T(8,128)(2,1)} %slice.183), channel_id=1, source_target_pairs={{4,0},{5,1},{6,2},{7,3},{12,8},{13,9},{14,10},{15,11},{20,16},{21,... | collective-permute-start | bytes 1572872 | tf_op jit(solution)/shard_map/ppermute | solution.py:16
  644.9 13.3 %collective-permute-start.2 = (bf16[1024,4,64]{0,2,1:T(8,128)(2,1)}, bf16[1024,4,64]{0,2,1:T(8,128)(2,1)}, u32[]{:S(2)}, u32[]{:S(2)}) collective-permute-start(bf16[1024,4,64]{0,2,1:T(8,128)(2,1)} %slice.184), channel_id=1, source_target_pairs={{4,0},{5,1},{6,2},{7,3},{12,8},{13,9},{14,10},{15,11},{20,16},{21,... | collective-permute-start | bytes 1572872 | tf_op jit(solution)/shard_map/ppermute | solution.py:16
  671.3 125.7 %all-gather.15.cloned.1.call-start = ((), (), s32[]{:S(2)}) async-start(), calls=%async_computation.14 | async-start | bytes 2621440 | tf_op jit(solution)/shard_map/all_gather | solution.py:52
  679.3 70.1 %copy-start.14 = (bf16[1,1,256,1024]{3,2,1,0:T(8,128)(2,1)S(1)}, bf16[1,1,256,1024]{3,2,1,0:T(8,128)(2,1)}, u32[]{:S(2)}) copy-start(bf16[1,1,256,1024]{3,2,1,0:T(8,128)(2,1)} %param.18) | copy-start | bytes 1572868
  679.3 70.1 %copy-start.55 = (f32[256]{0:T(256)S(1)}, f32[256]{0:T(256)}, u32[]{:S(2)}) copy-start(f32[256]{0:T(256)} %copy-done.54) | copy-start | bytes 3076
  679.3 70.1 %copy-start.59 = (f32[256]{0:T(256)S(1)}, f32[256]{0:T(256)}, u32[]{:S(2)}) copy-start(f32[256]{0:T(256)} %copy-done.58) | copy-start | bytes 3076
  679.3 138.7 %reduce-scatter.14.cloned.1.call-start = ((), (), s32[]{:S(2)}) async-start(), calls=%async_computation.13 | async-start | bytes 122880 | tf_op jit(solution)/shard_map/reduce_scatter | solution.py:322
  685.6 65.9 %copy-start.16 = (f32[256,1024]{1,0:T(8,128)S(1)}, f32[256,1024]{1,0:T(8,128)}, u32[]{:S(2)}) copy-start(f32[256,1024]{1,0:T(8,128)} %get-tuple-element.274) | copy-start | bytes 3145732
  758.7 200.6 %all-reduce.3.cloned.1.call-start = ((), (), s32[]{:S(2)}) async-start(), calls=%async_computation.16 | async-start | bytes 18874368 | tf_op jit(solution)/shard_map/psum | solution.py:330
  (71 other events, 726.1 us)
Sparse Core Ops, SparseCore 0:
  38.5 46.9 all-gather.6
  139.1 75.8 reduce-scatter.5
  221.0 46.1 all-gather.10
  268.6 44.4 all-gather.8
  329.0 75.5 reduce-scatter.9
  406.7 77.2 reduce-scatter.7
  488.9 46.1 all-gather.12
  536.7 44.4 all-gather.16
  671.4 77.9 reduce-scatter.11
  750.8 46.1 all-gather.14
  799.8 18.1 reduce-scatter.13
  822.9 136.2 all-reduce.2
where the time goes:
time: 991 us; the launch traced here: 982 us
  waiting for transfers between devices  623 us (63%)
  matrix products  156 us (16%)
  other arithmetic  102 us (10%)
  local copies, waits for them, and re-layouts  45.5 us (5%)
  blocking collectives  30.8 us (3%)
  between operations  16.1 us (2%)
    reduce_scatter x4, waiting for transfers between devices, collect_rows(): lax.psum_scatter(lax.dot_general(left_rows, right_matrix, (((1,), (contra...  282 us
    all_gather x6, waiting for transfers between devices, spread_rows(): return lax.all_gather(rows, 'tensor', axis=0, tiled=True)  202 us
    psum x1, waiting for transfers between devices, local(): lax.psum(grad_w_mod.astype(jnp.bfloat16), ('frames', 'batch'))  121 us
    dot_general x2, matrix products, attend_back(): jnp.einsum('qhd,khd->hqk', grad_mixed, all_values, preferred_element_type...  23.3 us
    convert_element_type x2, other arithmetic, attend_back(): grad_scores = (probabilities * (grad_probs - centre)).astype(jnp.bfloat16)  22 us
    dot_general x4, matrix products, collect_rows(): lax.dot_general(left_rows, right_matrix, (((1,), (contract,)), ((), ())),...  21.3 us
  transfers between devices with their start and end apart: 16, of which 11 were waited for; matrix products, arithmetic and copies ran while one was open for 20% of the time, Pallas kernels for 0%

commit v1 on v0

--- a/solution.py
+++ b/solution.py
@@ -327,7 +327,9 @@
     )
     grad_b_mod = jnp.sum(mod_share, axis=0)
     summed = (
-        lax.psum(grad_w_mod.astype(jnp.bfloat16), ("frames", "batch")).astype(jnp.float32),
+        jnp.sum(
+            lax.all_gather(grad_w_mod.astype(jnp.bfloat16), ("frames", "batch")), axis=0
+        ).astype(jnp.float32),
         lax.psum(grad_b_mod.astype(jnp.bfloat16), ("frames", "batch")).astype(jnp.float32),
         lax.psum(grad_w_qkv.astype(jnp.bfloat16), ("frames", "batch")).astype(jnp.float32),
         lax.psum(grad_w_out.astype(jnp.bfloat16), ("frames", "batch")).astype(jnp.float32),

time: 991 us -> 1090 us (1.100)
  waiting for transfers between devices: 623 us -> 706 us
  other arithmetic: 102 us -> 120 us
    all_gather x0 -> x1, waiting for transfers between devices: none -> 101 us  [local(): lax.all_gather(grad_w_mod.astype(jnp.bfloat16), ('frames', 'batch'))]
    psum x1, waiting for transfers between devices: 121 us -> 103 us  [local(): lax.psum(grad_w_qkv.astype(jnp.bfloat16), ('frames', 'batch'))]
    reduce_sum x0 -> x1, other arithmetic: none -> 15.7 us  [local(): jnp.sum(lax.all_gather(grad_w_mod.astype(jnp.bfloat16), ('frames', 'batch...]
  transfers between devices with their start and end apart: 16 -> 17, of which waited for: 11 -> 12; matrix products, arithmetic and copies ran while one was open for 20% -> 20% of each run, Pallas kernels for 0% -> 0%
where the time goes in v1:
time: 1090 us; the launch traced here: 1080 us
  waiting for transfers between devices  706 us (65%)
  matrix products  156 us (14%)
  other arithmetic  120 us (11%)
  local copies, waits for them, and re-layouts  44.3 us (4%)
  blocking collectives  30.8 us (3%)
  between operations  15.8 us (1%)
    reduce_scatter x4, waiting for transfers between devices, collect_rows(): lax.psum_scatter(lax.dot_general(left_rows, right_matrix, (((1,), (contra...  282 us
    all_gather x6, waiting for transfers between devices, spread_rows(): return lax.all_gather(rows, 'tensor', axis=0, tiled=True)  203 us
    psum x1, waiting for transfers between devices, local(): lax.psum(grad_w_qkv.astype(jnp.bfloat16), ('frames', 'batch'))  103 us
    all_gather x1, waiting for transfers between devices, local(): lax.all_gather(grad_w_mod.astype(jnp.bfloat16), ('frames', 'batch'))  101 us
    dot_general x2, matrix products, attend_back(): jnp.einsum('qhd,khd->hqk', grad_mixed, all_values, preferred_element_type...  23.2 us
    convert_element_type x2, other arithmetic, attend_back(): grad_scores = (probabilities * (grad_probs - centre)).astype(jnp.bfloat16)  22 us
  transfers between devices with their start and end apart: 17, of which 12 were waited for; matrix products, arithmetic and copies ran while one was open for 20% of the time, Pallas kernels for 0%

profile of v1, /device:TPU:0, one launch (start us, length us, event | category | flops | bytes accessed | tf_op | source)
XLA Modules:
  0.0 1080.5 jit_solution(15660146698962380537)
XLA Ops:
  16.0 15.6 %all_gather.27 = f32[8,6144]{1,0:T(8,128)S(1)} all-gather(f32[8,1536]{1,0:T(8,128)S(1)} %convolution_add_fusion), channel_id=1, replica_groups=mesh['tensor'=4,'frames'=2,'batch'=4] {'tensor'}, dimensions={1}, use_global_device_ids=true | all-gather | bytes 245760 | tf_op jit(solution)/shard_map/all_gather | solution.py:176
  51.3 34.1 %all-gather.9.cloned.1.call-done = bf16[1024,1024]{1,0:T(8,128)(2,1)} async-done(((bf16[256,1024]{1,0:T(8,128)(2,1)}), bf16[1024,1024]{1,0:T(8,128)(2,1)}) %all-gather.9.cloned.1.call-update) | async-done | bytes 2097168 | tf_op jit(solution)/shard_map/all_gather | solution.py:52
  104.5 29.2 %while.29 = (s32[]{:T(128)}, bf16[2,512,4,64]{1,3,2,0:T(8,128)(2,1)S(1)}, f32[2,4,512]{2,1,0:T(4,128)}, s32[2,512]{1,0:T(2,128)S(1)}, s32[2048]{0:T(1024)S(1)}, ...) while((s32[]{:T(128)}, ...), condition=%wide.region_5.7_spmd.clone, body=%wide.region_2.6_spmd.sunk.clone | while | flops 1127217152 | bytes 57503868 | solution.py:220
  139.0 75.9 %reduce-scatter.6.cloned.1.call-done = f32[256,1024]{1,0:T(8,128)} async-done(((f32[1024,1024]{1,0:T(8,128)}), f32[256,1024]{1,0:T(8,128)}) %reduce-scatter.6.cloned.1.call-update) | async-done | bytes 1048592 | tf_op jit(solution)/shard_map/reduce_scatter | solution.py:56
  221.9 45.3 %all-gather.13.cloned.1.call-done = bf16[1024,1024]{1,0:T(8,128)(2,1)} async-done(((bf16[256,1024]{1,0:T(8,128)(2,1)}), bf16[1024,1024]{1,0:T(8,128)(2,1)}) %all-gather.13.cloned.1.call-update) | async-done | bytes 2097168 | tf_op jit(solution)/shard_map/all_gather | solution.py:52
  273.8 39.3 %all-gather.11.cloned.1.call-done = bf16[1024,1024]{1,0:T(8,128)(2,1)} async-done(((bf16[256,1024]{1,0:T(8,128)(2,1)}), bf16[1024,1024]{1,0:T(8,128)(2,1)}) %all-gather.11.cloned.1.call-update) | async-done | bytes 2097168 | tf_op jit(solution)/shard_map/all_gather | solution.py:52
  313.1 10.0 fusion.47
  328.9 7.5 fusion.101
  336.5 68.1 %reduce-scatter.10.cloned.1.call-done = f32[256,1024]{1,0:T(8,128)} async-done(((f32[1024,1024]{1,0:T(8,128)}), f32[256,1024]{1,0:T(8,128)}) %reduce-scatter.10.cloned.1.call-update) | async-done | bytes 1048592 | tf_op jit(solution)/shard_map/reduce_scatter | solution.py:56
  406.9 77.3 %reduce-scatter.8.cloned.1.call-done = f32[256,1024]{1,0:T(8,128)} async-done(((f32[1024,1024]{1,0:T(8,128)}), f32[256,1024]{1,0:T(8,128)}) %reduce-scatter.8.cloned.1.call-update) | async-done | bytes 1048592 | tf_op jit(solution)/shard_map/reduce_scatter | solution.py:56
  489.6 45.5 %all-gather.15.cloned.1.call-done = bf16[1024,1024]{1,0:T(8,128)(2,1)} async-done(((bf16[256,1024]{1,0:T(8,128)(2,1)}), bf16[1024,1024]{1,0:T(8,128)(2,1)}) %all-gather.15.cloned.1.call-update) | async-done | bytes 2097168 | tf_op jit(solution)/shard_map/all_gather | solution.py:52
  541.2 94.7 %while.30 = (s32[]{:T(128)}, f32[2048,4,64]{0,2,1:T(8,128)}, f32[2048,4,64]{0,2,1:T(8,128)}, f32[2,512,4,64]{1,3,2,0:T(8,128)}, bf16[2,512,4,64]{1,3,2,0:T(8,128...) while((s32[]{:T(128)}, f32[2048,4,64]{0,2,1:T(8,128)}, ...), condition=%wide.region_15.17_spmd.clone.clone, body=%wide.region_13.16_spmd.clone.sunk.clone | while | flops 2753165312 | bytes 195776976 | solution.py:278
  554.4 11.6 %multiply_reduce_fusion.5 = (f32[4,512]{1,0:T(4,128)}, f32[4,512,2048]{2,1,0:T(8,128)}) fusion(f32[4,512,2048]{2,1,0:T(8,128)S(1)} %fusion.188, f32[4,512]{1,0:T(4,128)S(1)} %dynamic-slice_bitcast_fusion.3, pred[512,2048]{1,0:T(8,128)(4,1)} %copy-done.3, bf16[2048,4,64]{0,2,1:T(8,128)(2,1)} %copy-done.8, ...), kind=kOutput, calls=%fused_computation.20.clone.1.clone | convolution fusion | flops 557840384 | bytes 35930116 | tf_op jit(solution)/shard_map/while/body/eval_jaxpr/qhd,khd->hqk/dot_general | solution.py:112
  566.0 11.0 %multiply_convert_fusion.10 = bf16[4,512,2048]{2,1,0:T(8,128)(2,1)} fusion(f32[4,512,2048]{2,1,0:T(8,128)} %get-tuple-element.523, f32[4,512,2048]{2,1,0:T(8,128)S(1)} %fusion.188, f32[4,512]{1,0:T(4,128)} %get-tuple-element.524, f32[4,512]{1,0:T(4,128)S(1)} %dynamic-slice_bitcast_fusion.3, pred[512,2048]{1,0:T(8,128)(4,1)} %copy-done.3), kind=kLoop, calls=%fused_computation.19.clone.1.clone | loop fusion | flops 25165824 | bytes 43008000 | tf_op jit(solution)/shard_map/while/body/eval_jaxpr/convert_element_type | solution.py:116
  593.9 7.5 fusion.190
  601.4 11.6 %multiply_reduce_fusion.5 = (f32[4,512]{1,0:T(4,128)}, f32[4,512,2048]{2,1,0:T(8,128)}) fusion(f32[4,512,2048]{2,1,0:T(8,128)S(1)} %fusion.188, f32[4,512]{1,0:T(4,128)S(1)} %dynamic-slice_bitcast_fusion.3, pred[512,2048]{1,0:T(8,128)(4,1)} %copy-done.3, bf16[2048,4,64]{0,2,1:T(8,128)(2,1)} %copy-done.8, ...), kind=kOutput, calls=%fused_computation.20.clone.1.clone | convolution fusion | flops 557840384 | bytes 35930116 | tf_op jit(solution)/shard_map/while/body/eval_jaxpr/qhd,khd->hqk/dot_general | solution.py:112
  613.0 11.0 %multiply_convert_fusion.10 = bf16[4,512,2048]{2,1,0:T(8,128)(2,1)} fusion(f32[4,512,2048]{2,1,0:T(8,128)} %get-tuple-element.523, f32[4,512,2048]{2,1,0:T(8,128)S(1)} %fusion.188, f32[4,512]{1,0:T(4,128)} %get-tuple-element.524, f32[4,512]{1,0:T(4,128)S(1)} %dynamic-slice_bitcast_fusion.3, pred[512,2048]{1,0:T(8,128)(4,1)} %copy-done.3), kind=kLoop, calls=%fused_computation.19.clone.1.clone | loop fusion | flops 25165824 | bytes 43008000 | tf_op jit(solution)/shard_map/while/body/eval_jaxpr/convert_element_type | solution.py:116
  688.8 60.6 %reduce-scatter.12.cloned.1.call-done = f32[256,1024]{1,0:T(8,128)} async-done(((f32[1024,1024]{1,0:T(8,128)}), f32[256,1024]{1,0:T(8,128)}) %reduce-scatter.12.cloned.1.call-update) | async-done | bytes 1048592 | tf_op jit(solution)/shard_map/reduce_scatter | solution.py:56
  758.8 38.3 %all-gather.17.cloned.1.call-done = bf16[1024,1024]{1,0:T(8,128)(2,1)} async-done(((bf16[256,1024]{1,0:T(8,128)(2,1)}), bf16[1024,1024]{1,0:T(8,128)(2,1)}) %all-gather.17.cloned.1.call-update) | async-done | bytes 2097168 | tf_op jit(solution)/shard_map/all_gather | solution.py:52
  801.7 16.4 %reduce-scatter.14.cloned.1.call-done = bf16[8,1536]{1,0:T(8,128)(2,1)} async-done(((bf16[8,6144]{1,0:T(8,128)(2,1)}), bf16[8,1536]{1,0:T(8,128)(2,1)}) %reduce-scatter.14.cloned.1.call-update) | async-done | bytes 24592 | tf_op jit(solution)/shard_map/reduce_scatter | solution.py:322
  821.6 102.7 %all-reduce.3.cloned.1.call-done = (bf16[1024,3,256]{2,0,1:T(8,128)(2,1)}, bf16[256,1024]{1,0:T(8,128)(2,1)}, bf16[1024,1024]{1,0:T(8,128)(2,1)}, bf16[1024,1024]{1,0:T(8,128)(2,1)}) async-done(((bf16[1024,3,256]{2,0,1:T(8,128)(2,1)}, bf16[256,1024]{1,0:T(8,128)(2,1)}, bf16[1024,1024]{1,0:T(8,128)(2,1)}, bf16[1024,1024]{1,0:T(8,128)(2,1)}), (bf16[1024,3,256]{2,0,1:T(8,128)(2,1)}, ...) | async-done | bytes 6291472 | tf_op jit(solution)/shard_map/psum | solution.py:334
  935.4 15.2 %psum.35 = bf16[1536]{0:T(1024)(128)(2,1)S(1)} all-reduce(bf16[1536]{0:T(1024)(128)(2,1)S(1)} %reduce_sum.123), channel_id=1, replica_groups=mesh['tensor'=4,'frames'=2,'batch'=4] {'frames','batch'}, use_global_device_ids=true, to_apply=%region_22.24 | all-reduce | flops 1536 | bytes 6144 | tf_op jit(solution)/shard_map/psum | solution.py:333
  951.2 101.2 %all-gather.21.cloned.1.call-done = bf16[8192,1536]{1,0:T(8,128)(2,1)} async-done(((bf16[1024,1536]{1,0:T(8,128)(2,1)}), bf16[8192,1536]{1,0:T(8,128)(2,1)}) %all-gather.21.cloned.1.call-update) | async-done | bytes 25165840 | tf_op jit(solution)/shard_map/all_gather | solution.py:331
  1052.4 15.7 %reduce_sum.122 = bf16[1024,1536]{1,0:T(8,128)(2,1)} reduce(bf16[8,1024,1536]{2,1,0:T(8,128)(2,1)} %bitcast.244, bf16[]{:T(256)} %constant.152.clone.1), dimensions={0}, to_apply=%region_20.22 | reduce | flops 11010048 | bytes 28311554 | tf_op jit(solution)/shard_map/reduce_sum | solution.py:330
  (316 shorter events, 242.6 us)
Async XLA Ops:
  7.2 78.3 %all-gather.9.cloned.1.call-start = ((), (), s32[]{:S(2)}) async-start(), calls=%async_computation.5 | async-start | bytes 2621440 | tf_op jit(solution)/shard_map/all_gather | solution.py:52
  38.4 176.5 %reduce-scatter.6.cloned.1.call-start = ((), (), s32[]{:S(2)}) async-start(), calls=%async_computation.6 | async-start | bytes 5242880 | tf_op jit(solution)/shard_map/reduce_scatter | solution.py:56
  90.1 13.0 %collective-permute-start.1 = (bf16[1024,4,64]{0,2,1:T(8,128)(2,1)}, bf16[1024,4,64]{0,2,1:T(8,128)(2,1)}, u32[]{:S(2)}, u32[]{:S(2)}) collective-permute-start(bf16[1024,4,64]{0,2,1:T(8,128)(2,1)} %bitcast.31), channel_id=1, source_target_pairs={{0,4},{1,5},{2,6},{3,7},{8,12},{9,13},{10,14},{11,15},{16,20},{17,... | collective-permute-start | bytes 1572872 | tf_op jit(solution)/shard_map/ppermute | solution.py:16
  99.5 4.8 collective-permute-start
  138.9 76.0 %copy-start.13 = (bf16[1,1,256,1024]{3,2,1,0:T(8,128)(2,1)S(1)}, bf16[1,1,256,1024]{3,2,1,0:T(8,128)(2,1)}, u32[]{:S(2)}) copy-start(bf16[1,1,256,1024]{3,2,1,0:T(8,128)(2,1)} %param.18) | copy-start | bytes 1572868
  138.9 128.3 %all-gather.13.cloned.1.call-start = ((), (), s32[]{:S(2)}) async-start(), calls=%async_computation.9 | async-start | bytes 2621440 | tf_op jit(solution)/shard_map/all_gather | solution.py:52
  216.7 267.4 %copy-start.50 = (f32[256]{0:T(256)}, f32[256]{0:T(256)S(1)}, u32[]{:S(2)}) copy-start(f32[256]{0:T(256)S(1)} %broadcast_multiply_fusion.4) | copy-start | bytes 3076
  217.7 266.4 %copy-start.55 = (f32[256]{0:T(256)}, f32[256]{0:T(256)S(1)}, u32[]{:S(2)}) copy-start(f32[256]{0:T(256)S(1)} %add_rsqrt_fusion) | copy-start | bytes 3076
  220.8 92.3 %all-gather.11.cloned.1.call-start = ((), (), s32[]{:S(2)}) async-start(), calls=%async_computation.7 | async-start | bytes 2621440 | tf_op jit(solution)/shard_map/all_gather | solution.py:52
  221.4 183.2 %reduce-scatter.10.cloned.1.call-start = ((), (), s32[]{:S(2)}) async-start(), calls=%async_computation.10 | async-start | bytes 5242880 | tf_op jit(solution)/shard_map/reduce_scatter | solution.py:56
  328.9 155.2 %reduce-scatter.8.cloned.1.call-start = ((), (), s32[]{:S(2)}) async-start(), calls=%async_computation.8 | async-start | bytes 5242880 | tf_op jit(solution)/shard_map/reduce_scatter | solution.py:56
  336.4 147.7 %copy-start.19 = (bf16[1,1,256,1024]{3,2,1,0:T(8,128)(2,1)S(1)}, bf16[1,1,256,1024]{3,2,1,0:T(8,128)(2,1)}, u32[]{:S(2)}) copy-start(bf16[1,1,256,1024]{3,2,1,0:T(8,128)(2,1)} %param.19) | copy-start | bytes 1572868
  336.4 198.7 %all-gather.15.cloned.1.call-start = ((), (), s32[]{:S(2)}) async-start(), calls=%async_computation.11 | async-start | bytes 2621440 | tf_op jit(solution)/shard_map/all_gather | solution.py:52
  488.8 190.8 %all-gather.19.cloned.1.call-start = ((), (), s32[]{:S(2)}) async-start(), calls=%async_computation.15 | async-start | bytes 2621440 | tf_op jit(solution)/shard_map/all_gather | solution.py:52
  489.6 259.8 %reduce-scatter.12.cloned.1.call-start = ((), (), s32[]{:S(2)}) async-start(), calls=%async_computation.12 | async-start | bytes 5242880 | tf_op jit(solution)/shard_map/reduce_scatter | solution.py:56
  638.2 15.6 %collective-permute-start.3 = (bf16[1024,4,64]{0,2,1:T(8,128)(2,1)}, bf16[1024,4,64]{0,2,1:T(8,128)(2,1)}, u32[]{:S(2)}, u32[]{:S(2)}) collective-permute-start(bf16[1024,4,64]{0,2,1:T(8,128)(2,1)} %slice.183), channel_id=1, source_target_pairs={{4,0},{5,1},{6,2},{7,3},{12,8},{13,9},{14,10},{15,11},{20,16},{21,... | collective-permute-start | bytes 1572872 | tf_op jit(solution)/shard_map/ppermute | solution.py:16
  644.9 13.3 %collective-permute-start.2 = (bf16[1024,4,64]{0,2,1:T(8,128)(2,1)}, bf16[1024,4,64]{0,2,1:T(8,128)(2,1)}, u32[]{:S(2)}, u32[]{:S(2)}) collective-permute-start(bf16[1024,4,64]{0,2,1:T(8,128)(2,1)} %slice.184), channel_id=1, source_target_pairs={{4,0},{5,1},{6,2},{7,3},{12,8},{13,9},{14,10},{15,11},{20,16},{21,... | collective-permute-start | bytes 1572872 | tf_op jit(solution)/shard_map/ppermute | solution.py:16
  671.3 125.7 %all-gather.17.cloned.1.call-start = ((), (), s32[]{:S(2)}) async-start(), calls=%async_computation.14 | async-start | bytes 2621440 | tf_op jit(solution)/shard_map/all_gather | solution.py:52
  679.3 70.1 %copy-start.14 = (bf16[1,1,256,1024]{3,2,1,0:T(8,128)(2,1)S(1)}, bf16[1,1,256,1024]{3,2,1,0:T(8,128)(2,1)}, u32[]{:S(2)}) copy-start(bf16[1,1,256,1024]{3,2,1,0:T(8,128)(2,1)} %param.18) | copy-start | bytes 1572868
  679.3 70.1 %copy-start.54 = (f32[256]{0:T(256)S(1)}, f32[256]{0:T(256)}, u32[]{:S(2)}) copy-start(f32[256]{0:T(256)} %copy-done.53) | copy-start | bytes 3076
  679.3 70.1 %copy-start.58 = (f32[256]{0:T(256)S(1)}, f32[256]{0:T(256)}, u32[]{:S(2)}) copy-start(f32[256]{0:T(256)} %copy-done.57) | copy-start | bytes 3076
  679.4 138.7 %reduce-scatter.14.cloned.1.call-start = ((), (), s32[]{:S(2)}) async-start(), calls=%async_computation.13 | async-start | bytes 122880 | tf_op jit(solution)/shard_map/reduce_scatter | solution.py:322
  758.7 165.6 %all-reduce.3.cloned.1.call-start = ((), (), s32[]{:S(2)}) async-start(), calls=%async_computation.17 | async-start | bytes 12582912 | tf_op jit(solution)/shard_map/psum | solution.py:334
  801.7 250.7 %all-gather.21.cloned.1.call-start = ((), (), s32[]{:S(2)}) async-start(), calls=%async_computation.16 | async-start | bytes 28311552 | tf_op jit(solution)/shard_map/all_gather | solution.py:331
  (71 other events, 721.5 us)
Sparse Core Ops, SparseCore 0:
  38.5 46.9 all-gather.8
  139.0 75.8 reduce-scatter.5
  220.9 46.1 all-gather.12
  268.6 44.4 all-gather.10
  329.0 75.5 reduce-scatter.9
  406.8 77.2 reduce-scatter.7
  489.0 46.1 all-gather.14
  536.7 44.4 all-gather.18
  671.5 77.9 reduce-scatter.11
  750.8 46.1 all-gather.16
  799.8 18.1 reduce-scatter.13
  822.1 102.1 all-reduce.2
  926.8 125.5 all-gather.20
